TPU v7x, 256 devices: a whole 4x4x8 slice. The times are simulated.
256 devices in a mesh: group: 16 (over z, core), blk: 16 (over y, x).
Axes of the slice: x: 4, y: 4, z: 8, core: 2. Of those that a mesh axis runs over, the one named last changes fastest.
Arguments:
- hamiltonian: bfloat16 [4096, 18, 64, 256], P(('group', 'blk')), may hold values from -0.09375 to 0.09375
- block_columns: int32 [4096, 18, 4], P(('group', 'blk')), may hold values from 0 to 15, as said below
- potential: float32 [262144], P(('group', 'blk')), may hold values from -1 to 1
- trial_slab: float32 [262144, 128], P(('group', 'blk')), may hold values from -40 to 40
Outputs:
- ortho_slab: float32 [262144, 128], P(('group', 'blk'))
- upper_factor: float32 [128, 128], replicated
Inputs may be any that keep to these rules, and one draw needn't show every extreme that they name: `block_columns`: for each row block and each source, the 4 entries are distinct.
All inputs are finite; a program needn't handle non-finite values.
Results may differ from a plain program's by a relative error of at most 0.0021.
Values may be sent and summed in bfloat16 or wider, within the bound.
A program may use at most 64 MiB of HBM per device.

v0:
```python
import jax
import jax.numpy as jnp
from jax import lax
from jax.sharding import PartitionSpec as P

precise = lax.Precision.HIGHEST


def neighbours(block):
    count = lax.axis_size("group")
    forward = [(i, i + 1) for i in range(count - 1)]
    backward = [(i + 1, i) for i in range(count - 1)]
    below = lax.ppermute(block, "group", forward)
    above = lax.ppermute(block, "group", backward)
    return (below, above)


def couple_all(hamiltonian, block_columns, rounded):
    shard_blocks, nsrc, block_size, width = hamiltonian.shape
    per_source = block_columns.shape[2]
    states = rounded.shape[2]
    gathered = lax.all_gather(rounded, "blk", axis=0, tiled=True)
    below, above = neighbours(rounded)
    table = jnp.concatenate([gathered, below, above], axis=0)
    offsets = (jnp.arange(nsrc, dtype=jnp.int32) * shard_blocks)[None, :, None]
    index = block_columns + offsets
    picked = table[index.reshape(-1)].reshape(shard_blocks, nsrc, per_source * block_size, states)
    return jnp.einsum("rsik,rskn->rin", hamiltonian, picked, preferred_element_type=jnp.float32)


def on_device(hamiltonian, block_columns, potential, trial_slab):
    shard_blocks = hamiltonian.shape[0]
    block_size = hamiltonian.shape[2]
    states = trial_slab.shape[1]
    start_slab = trial_slab.reshape(shard_blocks, block_size, states)
    weights = potential.reshape(shard_blocks, block_size, 1)
    coupled_start = couple_all(hamiltonian, block_columns, start_slab.astype(jnp.bfloat16))
    filtered_once = 0.5 * (coupled_start + weights * start_slab)
    coupled_next = couple_all(hamiltonian, block_columns, filtered_once.astype(jnp.bfloat16))
    filtered = coupled_next + weights * filtered_once - start_slab
    flat = filtered.reshape(shard_blocks * block_size, states)
    rows_total = flat.shape[0] * lax.axis_size("group") * lax.axis_size("blk")
    local_gram = jnp.dot(flat.T, flat, precision=precise)
    gram = lax.psum(local_gram, ("group", "blk")) / rows_total
    lower = jnp.linalg.cholesky(gram)
    ortho_slab = lax.linalg.triangular_solve(
        lower, flat, left_side=False, lower=True, transpose_a=True
    )
    return (ortho_slab, jnp.transpose(lower))


def solution(mesh):
    placed = (
        P(("group", "blk"), None, None, None),
        P(("group", "blk"), None, None),
        P(("group", "blk")),
        P(("group", "blk"), None),
    )
    return jax.shard_map(
        on_device,
        mesh=mesh,
        in_specs=placed,
        out_specs=(P(("group", "blk"), None), P()),
        check_vma=False,
    )
```

profile of v0, /device:TPU:1, one launch (start us, length us, event | category | flops | bytes accessed | tf_op | source)
XLA Modules:
  0.0 493.7 jit_solution(8105677238921476546)
XLA Ops:
  7.2 1.8 convert_element_type.6
  9.1 5.1 %collective-permute-start.1 = (bf16[16,64,128]{2,1,0:T(8,128)(2,1)}, bf16[16,64,128]{2,1,0:T(8,128)(2,1)S(1)}, u32[]{:S(2)}, u32[]{:S(2)}) collective-permute-start(bf16[16,64,128]{2,1,0:T(8,128)(2,1)} %convert_element_type.6), channel_id=1, source_target_pairs={{16,0},{32,16},{48,32},{64,48},{80,64},{96,80},{112,96},{128,112},... | collective-permute-start | bytes 786440 | tf_op jit(solution)/shard_map/ppermute | solution.py:14
  14.2 1.9 collective-permute-start
  16.2 0.8 broadcast_add_fusion
  16.9 0.8 mul.37
  17.7 0.2 copy.13
  17.9 0.1 reshape.64
  18.1 0.2 collective-permute-done.1
  18.3 1.5 collective-permute-done
  19.8 51.6 %all-gather.3.cloned.1.call-done = bf16[256,64,128]{2,1,0:T(8,128)(2,1)} async-done(((bf16[16,64,128]{2,1,0:T(8,128)(2,1)}), bf16[256,64,128]{2,1,0:T(8,128)(2,1)}) %all-gather.3.cloned.1.call-update) | async-done | bytes 4194320 | tf_op jit(solution)/shard_map/all_gather | solution.py:22
  71.4 4.2 pad_maximum_fusion
  75.5 29.1 %gather_fusion = bf16[1152,64,128]{2,1,0:T(8,128)(2,1)} fusion(bf16[288,64,128]{2,1,0:T(8,128)(2,1)} %pad_maximum_fusion, s32[2048]{0:T(1024)S(1)} %pad_clamp_fusion), kind=kCustom, calls=%fused_computation | custom fusion | bytes 37753344 | tf_op jit(solution)/shard_map/gather | solution.py:27
  104.6 13.5 %multiply_convert_fusion = (bf16[16,64,128]{2,1,0:T(8,128)(2,1)}, f32[16,64,128]{2,1,0:T(8,128)S(1)}) fusion(f32[16,64,128]{2,1,0:T(8,128)S(1)} %bitcast.44, f32[16,64]{1,0:T(8,128)S(1)} %mul.37, bf16[16,18,64,256]{3,2,1,0:T(8,128)(2,1)} %param.4, bf16[16,18,256,128]{3,2,1,0:T(8,128)(2,1)} %bitcast.41), kind=kOutput, calls=%fused_computation.10 | convolution fusion | flops 1208483840 | bytes 29626368 | tf_op jit(solution)/shard_map/rsik,rskn->rin/dot_general | solution.py:28
  118.2 2.6 collective-permute-start.3
  120.8 3.3 collective-permute-start.2
  124.1 2.1 collective-permute-done.3
  126.2 1.3 collective-permute-done.2
  127.5 47.1 %all-gather.5.cloned.1.call-done = bf16[256,64,128]{2,1,0:T(8,128)(2,1)} async-done(((bf16[16,64,128]{2,1,0:T(8,128)(2,1)}), bf16[256,64,128]{2,1,0:T(8,128)(2,1)}) %all-gather.5.cloned.1.call-update) | async-done | bytes 4194320 | tf_op jit(solution)/shard_map/all_gather | solution.py:22
  174.6 4.2 pad_maximum_fusion.1
  178.8 29.2 %gather_fusion.1 = bf16[1152,64,128]{2,1,0:T(8,128)(2,1)} fusion(bf16[288,64,128]{2,1,0:T(8,128)(2,1)} %pad_maximum_fusion.1, s32[2048]{0:T(1024)S(1)} %pad_clamp_fusion), kind=kCustom, calls=%fused_computation.1 | custom fusion | bytes 37753344 | tf_op jit(solution)/shard_map/gather | solution.py:27
  208.0 12.8 %fusion.2 = f32[16,64,128]{2,1,0:T(8,128)S(1)} fusion(f32[16,64,128]{2,1,0:T(8,128)S(1)} %bitcast.45, bf16[16,18,64,256]{3,2,1,0:T(8,128)(2,1)} %param.4, bf16[16,18,256,128]{3,2,1,0:T(8,128)(2,1)} %bitcast.40, f32[16,64,128]{2,1,0:T(8,128)S(1)} %get-tuple-element.11, f32[16,64]{1,0:T(8,128)S(1)} %broadcast_multiply_fusion.1), kind=kOutput, calls=%fused_computation.8 | convolution fusion | flops 1208352768 | bytes 29888512 | tf_op jit(solution)/shard_map/rsik,rskn->rin/dot_general | solution.py:28
  220.8 1.6 convolution_bitcast_fusion.2
  222.5 237.9 %all-reduce.2.cloned.1.call-done = f32[128,128]{0,1:T(8,128)} async-done(((f32[128,128]{0,1:T(8,128)}), f32[128,128]{0,1:T(8,128)}) %all-reduce.2.cloned.1.call-update) | async-done | bytes 65552 | tf_op jit(solution)/shard_map/psum | solution.py:44
  460.4 0.8 broadcast_multiply_fusion
  461.3 0.1 copy.15
  461.4 0.9 fusion.5
  462.2 11.7 %cholesky.16 = f32[128,128]{1,0:T(8,128)S(1)} custom-call(f32[128,128]{1,0:T(8,128)S(1)} %fusion.5), custom_call_target="Cholesky" | custom-call | tf_op jit(solution)/shard_map/jit(cholesky)/cholesky | solution.py:45
  474.0 0.6 compare_reduce_fusion
  474.6 0.7 fusion.6
  475.3 0.7 copy.16
  476.0 9.8 %custom-call.6 = f32[1,128,128]{1,2,0:T(8,128)S(1)} custom-call(f32[1,128,128]{2,1,0:T(8,128)S(1)} %get-tuple-element.9), custom_call_target="InvertDiagBlocksLowerTriangular" | custom-call | tf_op jit(solution)/shard_map/triangular_solve | solution.py:46
  485.8 1.4 fusion.3
  (13 shorter events, 0.2 us)
Async XLA Ops:
  7.2 64.2 %all-gather.3.cloned.1.call-start = ((), (), s32[]{:S(2)}) async-start(), calls=%async_computation | async-start | bytes 4456448 | tf_op jit(solution)/shard_map/all_gather | solution.py:22
  9.0 165.6 %all-gather.5.cloned.1.call-start = ((), (), s32[]{:S(2)}) async-start(), calls=%async_computation.1 | async-start | bytes 4456448 | tf_op jit(solution)/shard_map/all_gather | solution.py:22
  9.1 9.2 %collective-permute-start.1 = (bf16[16,64,128]{2,1,0:T(8,128)(2,1)}, bf16[16,64,128]{2,1,0:T(8,128)(2,1)S(1)}, u32[]{:S(2)}, u32[]{:S(2)}) collective-permute-start(bf16[16,64,128]{2,1,0:T(8,128)(2,1)} %convert_element_type.6), channel_id=1, source_target_pairs={{16,0},{32,16},{48,32},{64,48},{80,64},{96,80},{112,96},{128,112},... | collective-permute-start | bytes 786440 | tf_op jit(solution)/shard_map/ppermute | solution.py:14
  14.2 5.5 %collective-permute-start = (bf16[16,64,128]{2,1,0:T(8,128)(2,1)}, bf16[16,64,128]{2,1,0:T(8,128)(2,1)S(1)}, u32[]{:S(2)}, u32[]{:S(2)}) collective-permute-start(bf16[16,64,128]{2,1,0:T(8,128)(2,1)} %convert_element_type.6), channel_id=1, source_target_pairs={{0,16},{16,32},{32,48},{48,64},{64,80},{80,96},{96,112},{112,128},... | collective-permute-start | bytes 786440 | tf_op jit(solution)/shard_map/ppermute | solution.py:13
  75.5 29.1 %copy-start = (f32[1024,128]{1,0:T(8,128)S(1)}, f32[1024,128]{1,0:T(8,128)}, u32[]{:S(2)}) copy-start(f32[1024,128]{1,0:T(8,128)} %param.7) | copy-start | bytes 1572868
  118.2 342.3 %all-reduce.2.cloned.1.call-start = ((), (), s32[]{:S(2)}) async-start(), calls=%async_computation.2 | async-start | bytes 131072 | tf_op jit(solution)/shard_map/psum | solution.py:44
  118.2 8.0 %collective-permute-start.3 = (bf16[16,64,128]{2,1,0:T(8,128)(2,1)}, bf16[16,64,128]{2,1,0:T(8,128)(2,1)S(1)}, u32[]{:S(2)}, u32[]{:S(2)}) collective-permute-start(bf16[16,64,128]{2,1,0:T(8,128)(2,1)} %get-tuple-element.10), channel_id=1, source_target_pairs={{16,0},{32,16},{48,32},{64,48},{80,64},{96,80},{112,96},{128,112},... | collective-permute-start | bytes 786440 | tf_op jit(solution)/shard_map/ppermute | solution.py:14
  120.8 6.7 %collective-permute-start.2 = (bf16[16,64,128]{2,1,0:T(8,128)(2,1)}, bf16[16,64,128]{2,1,0:T(8,128)(2,1)S(1)}, u32[]{:S(2)}, u32[]{:S(2)}) collective-permute-start(bf16[16,64,128]{2,1,0:T(8,128)(2,1)} %get-tuple-element.10), channel_id=1, source_target_pairs={{0,16},{16,32},{32,48},{48,64},{64,80},{80,96},{96,112},{112,128},... | collective-permute-start | bytes 786440 | tf_op jit(solution)/shard_map/ppermute | solution.py:13
Sparse Core Ops, SparseCore 0:
  11.0 60.3 all-gather.2
  118.3 56.2 all-gather.4
  222.6 237.7 all-reduce.1
where the time goes:
time: 494 us
  waiting for transfers between devices  342 us (69%)
  local copies, waits for them, and re-layouts  60.2 us (12%)
  other arithmetic  35.5 us (7%)
  matrix products  29.3 us (6%)
  between operations  13.9 us (3%)
  starting transfers between devices  13 us (3%)
    psum x1, waiting for transfers between devices, on_device(): gram = lax.psum(local_gram, ('group', 'blk')) / rows_total  238 us
    all_gather x2, waiting for transfers between devices, couple_all(): gathered = lax.all_gather(rounded, 'blk', axis=0, tiled=True)  98.7 us
    gather x2, local copies, waits for them, and re-layouts, couple_all(): table[index.reshape(-1)]  58.3 us
    dot_general x2, matrix products, couple_all(): jnp.einsum('rsik,rskn->rin', hamiltonian, picked, preferred_element_type=...  26.3 us
    another operation x3, other arithmetic, on_device(): lower = jnp.linalg.cholesky(gram)  12.4 us
  transfers between devices with their start and end apart: 7, of which 7 were waited for; matrix products, arithmetic and copies ran while one was open for 0% of the time, Pallas kernels for 0%

commit v1 on v0

--- a/solution.py
+++ b/solution.py
@@ -4,6 +4,11 @@
 from jax.sharding import PartitionSpec as P
 
 precise = lax.Precision.HIGHEST
+
+
+def all_by_exchange(array, mesh_axis, dim):
+    outgoing = jnp.stack([array] * lax.axis_size(mesh_axis))
+    return jnp.concatenate(lax.all_to_all(outgoing, mesh_axis, 0, 0), axis=dim)
 
 
 def neighbours(block):
@@ -19,7 +24,7 @@
     shard_blocks, nsrc, block_size, width = hamiltonian.shape
     per_source = block_columns.shape[2]
     states = rounded.shape[2]
-    gathered = lax.all_gather(rounded, "blk", axis=0, tiled=True)
+    gathered = all_by_exchange(rounded, "blk", 0)
     below, above = neighbours(rounded)
     table = jnp.concatenate([gathered, below, above], axis=0)
     offsets = (jnp.arange(nsrc, dtype=jnp.int32) * shard_blocks)[None, :, None]

time: 494 us -> 517 us (1.047)
  starting transfers between devices: 13 us -> 26 us
  waiting for transfers between devices: 342 us -> 348 us
  local copies, waits for them, and re-layouts: 60.2 us -> 65.6 us
    all_to_all x0 -> x2, waiting for transfers between devices: none -> 102 us  [all_by_exchange(): return jnp.concatenate(lax.all_to_all(outgoing, mesh_axis, 0, 0), axis=dim)]
    all_gather x2 -> x0, waiting for transfers between devices: 98.7 us -> none  [couple_all(): gathered = lax.all_gather(rounded, 'blk', axis=0, tiled=True)]
    all_to_all x0 -> x2, starting transfers between devices: none -> 12.2 us  [all_by_exchange(): return jnp.concatenate(lax.all_to_all(outgoing, mesh_axis, 0, 0), axis=dim)]
    another operation x0 -> x2, local copies, waits for them, and re-layouts: none -> 6.06 us  [all_by_exchange(): outgoing = jnp.stack([array] * lax.axis_size(mesh_axis))]
where the time goes in v1:
time: 517 us; the launch traced here: 516 us
  waiting for transfers between devices  348 us (67%)
  local copies, waits for them, and re-layouts  65.6 us (13%)
  other arithmetic  34 us (7%)
  matrix products  28.6 us (6%)
  starting transfers between devices  26 us (5%)
  between operations  14.2 us (3%)
    psum x1, waiting for transfers between devices, on_device(): gram = lax.psum(local_gram, ('group', 'blk')) / rows_total  240 us
    all_to_all x2, waiting for transfers between devices, all_by_exchange(): return jnp.concatenate(lax.all_to_all(outgoing, mesh_axis, 0, 0), axis=dim)  102 us
    gather x2, local copies, waits for them, and re-layouts, couple_all(): table[index.reshape(-1)]  58.3 us
    dot_general x2, matrix products, couple_all(): jnp.einsum('rsik,rskn->rin', hamiltonian, picked, preferred_element_type=...  25.7 us
    another operation x3, other arithmetic, on_device(): lower = jnp.linalg.cholesky(gram)  12.4 us
    all_to_all x2, starting transfers between devices, all_by_exchange(): return jnp.concatenate(lax.all_to_all(outgoing, mesh_axis, 0, 0), axis=dim)  12.2 us
  transfers between devices with their start and end apart: 7, of which 7 were waited for; matrix products, arithmetic and copies ran while one was open for 0% of the time, Pallas kernels for 0%

profile of v1, /device:TPU:1, one launch (start us, length us, event | category | flops | bytes accessed | tf_op | source)
XLA Modules:
  0.0 516.1 jit_solution(8085434799348565124)
XLA Ops:
  7.2 1.1 convert_element_type.8
  8.3 3.0 stack.4
  11.3 7.6 %all-to-all-start = ((bf16[16,16,64,128]{3,2,1,0:T(8,128)(2,1)}), bf16[16,16,64,128]{3,2,1,0:T(8,128)(2,1)}, u32[]{:S(2)}, u32[]{:S(2)}) async-start(bf16[16,16,64,128]{3,2,1,0:T(8,128)(2,1)} %stack.4), calls=%async_computation | async-start | bytes 8388608 | tf_op jit(solution)/shard_map/all_to_all | solution.py:11
  19.0 2.9 collective-permute-start.1
  21.8 3.4 collective-permute-start
  25.4 0.2 copy.9
  25.8 2.0 collective-permute-done.1
  27.8 0.8 collective-permute-done
  28.6 52.7 %all-to-all-done = bf16[16,16,64,128]{3,2,1,0:T(8,128)(2,1)} async-done(((bf16[16,16,64,128]{3,2,1,0:T(8,128)(2,1)}), bf16[16,16,64,128]{3,2,1,0:T(8,128)(2,1)}, u32[]{:S(2)}, u32[]{:S(2)}) %all-to-all-start) | async-done | bytes 4194336 | tf_op jit(solution)/shard_map/all_to_all | solution.py:11
  81.3 4.2 pad_maximum_fusion
  85.5 29.1 %gather_fusion = bf16[1152,64,128]{2,1,0:T(8,128)(2,1)} fusion(bf16[288,64,128]{2,1,0:T(8,128)(2,1)} %pad_maximum_fusion, s32[2048]{0:T(1024)S(1)} %pad_clamp_fusion), kind=kCustom, calls=%fused_computation | custom fusion | bytes 37753344 | tf_op jit(solution)/shard_map/gather | solution.py:32
  114.6 12.8 %multiply_convert_fusion = (bf16[16,64,128]{2,1,0:T(8,128)(2,1)S(1)}, f32[16,64,128]{2,1,0:T(8,128)S(1)}) fusion(f32[16,64,128]{2,1,0:T(8,128)S(1)} %bitcast.46, f32[16,64]{1,0:T(8,128)S(1)} %mul.37, bf16[16,18,64,256]{3,2,1,0:T(8,128)(2,1)} %param.4, bf16[16,18,256,128]{3,2,1,0:T(8,128)(2,1)} %bitcast.43), kind=kOutput, calls=%fused_computation.10 | convolution fusion | flops 1208483840 | bytes 29626368 | tf_op jit(solution)/shard_map/rsik,rskn->rin/dot_general | solution.py:33
  127.4 3.0 stack.5
  130.4 4.5 all-to-all-start.1
  135.0 3.8 collective-permute-start.3
  138.8 3.6 collective-permute-start.2
  142.5 2.3 collective-permute-done.3
  144.8 0.8 collective-permute-done.2
  145.6 48.8 %all-to-all-done.1 = bf16[16,16,64,128]{3,2,1,0:T(8,128)(2,1)} async-done(((bf16[16,16,64,128]{3,2,1,0:T(8,128)(2,1)}), bf16[16,16,64,128]{3,2,1,0:T(8,128)(2,1)}, u32[]{:S(2)}, u32[]{:S(2)}) %all-to-all-start.1) | async-done | bytes 4194336 | tf_op jit(solution)/shard_map/all_to_all | solution.py:11
  194.4 4.2 pad_maximum_fusion.1
  198.6 29.2 %gather_fusion.1 = bf16[1152,64,128]{2,1,0:T(8,128)(2,1)} fusion(bf16[288,64,128]{2,1,0:T(8,128)(2,1)} %pad_maximum_fusion.1, s32[2048]{0:T(1024)S(1)} %pad_clamp_fusion), kind=kCustom, calls=%fused_computation.1 | custom fusion | bytes 37753344 | tf_op jit(solution)/shard_map/gather | solution.py:32
  227.8 12.8 %fusion.2 = f32[16,64,128]{2,1,0:T(8,128)S(1)} fusion(f32[16,64,128]{2,1,0:T(8,128)S(1)} %bitcast.47, bf16[16,18,64,256]{3,2,1,0:T(8,128)(2,1)} %param.4, bf16[16,18,256,128]{3,2,1,0:T(8,128)(2,1)} %bitcast.42, f32[16,64,128]{2,1,0:T(8,128)S(1)} %get-tuple-element.9, f32[16,64]{1,0:T(8,128)S(1)} %broadcast_multiply_fusion.1), kind=kOutput, calls=%fused_computation.8 | convolution fusion | flops 1208352768 | bytes 29888512 | tf_op jit(solution)/shard_map/rsik,rskn->rin/dot_general | solution.py:33
  240.6 1.6 convolution_bitcast_fusion.2
  242.3 240.2 %all-reduce.2.cloned.1.call-done = f32[128,128]{0,1:T(8,128)} async-done(((f32[128,128]{0,1:T(8,128)}), f32[128,128]{0,1:T(8,128)}) %all-reduce.2.cloned.1.call-update) | async-done | bytes 65552 | tf_op jit(solution)/shard_map/psum | solution.py:49
  482.5 0.8 broadcast_multiply_fusion
  483.5 0.9 fusion.5
  484.3 11.7 %cholesky.16 = f32[128,128]{1,0:T(8,128)S(1)} custom-call(f32[128,128]{1,0:T(8,128)S(1)} %fusion.5), custom_call_target="Cholesky" | custom-call | tf_op jit(solution)/shard_map/jit(cholesky)/cholesky | solution.py:50
  496.1 0.6 compare_reduce_fusion
  496.7 0.7 fusion.6
  497.4 0.7 copy.12
  498.1 9.8 %custom-call.6 = f32[1,128,128]{1,2,0:T(8,128)S(1)} custom-call(f32[1,128,128]{2,1,0:T(8,128)S(1)} %get-tuple-element.7), custom_call_target="InvertDiagBlocksLowerTriangular" | custom-call | tf_op jit(solution)/shard_map/triangular_solve | solution.py:51
  507.9 1.4 fusion.3
  (17 shorter events, 0.4 us)
Async XLA Ops:
  7.2 18.1 %copy-start.1 = (s32[16,18,4]{1,2,0:T(4,128)S(1)}, s32[16,18,4]{1,2,0:T(4,128)}, u32[]{:S(2)}) copy-start(s32[16,18,4]{1,2,0:T(4,128)} %param.5) | copy-start | bytes 13828
  7.2 18.1 %copy-start.2 = (f32[1024]{0:T(1024)S(1)}, f32[1024]{0:T(1024)}, u32[]{:S(2)}) copy-start(f32[1024]{0:T(1024)} %param.6) | copy-start | bytes 12292
  11.3 70.0 %all-to-all-start = ((bf16[16,16,64,128]{3,2,1,0:T(8,128)(2,1)}), bf16[16,16,64,128]{3,2,1,0:T(8,128)(2,1)}, u32[]{:S(2)}, u32[]{:S(2)}) async-start(bf16[16,16,64,128]{3,2,1,0:T(8,128)(2,1)} %stack.4), calls=%async_computation | async-start | bytes 8388608 | tf_op jit(solution)/shard_map/all_to_all | solution.py:11
  19.0 8.8 %collective-permute-start.1 = (bf16[16,64,128]{2,1,0:T(8,128)(2,1)S(1)}, bf16[16,64,128]{2,1,0:T(8,128)(2,1)S(1)}, u32[]{:S(2)}, u32[]{:S(2)}) collective-permute-start(bf16[16,64,128]{2,1,0:T(8,128)(2,1)S(1)} %convert_element_type.8), channel_id=1, source_target_pairs={{16,0},{32,16},{48,32},{64,48},{80,64},{96,80},{112,96},{128,112},... | collective-permute-start | bytes 786440 | tf_op jit(solution)/shard_map/ppermute | solution.py:19
  21.8 6.7 %collective-permute-start = (bf16[16,64,128]{2,1,0:T(8,128)(2,1)S(1)}, bf16[16,64,128]{2,1,0:T(8,128)(2,1)S(1)}, u32[]{:S(2)}, u32[]{:S(2)}) collective-permute-start(bf16[16,64,128]{2,1,0:T(8,128)(2,1)S(1)} %convert_element_type.8), channel_id=1, source_target_pairs={{0,16},{16,32},{32,48},{48,64},{64,80},{80,96},{96,112},{112,128},... | collective-permute-start | bytes 786440 | tf_op jit(solution)/shard_map/ppermute | solution.py:18
  85.5 29.1 %copy-start = (f32[1024,128]{1,0:T(8,128)S(1)}, f32[1024,128]{1,0:T(8,128)}, u32[]{:S(2)}) copy-start(f32[1024,128]{1,0:T(8,128)} %param.7) | copy-start | bytes 1572868
  130.4 64.0 %all-to-all-start.1 = ((bf16[16,16,64,128]{3,2,1,0:T(8,128)(2,1)}), bf16[16,16,64,128]{3,2,1,0:T(8,128)(2,1)}, u32[]{:S(2)}, u32[]{:S(2)}) async-start(bf16[16,16,64,128]{3,2,1,0:T(8,128)(2,1)} %stack.5), calls=%async_computation.1 | async-start | bytes 8388608 | tf_op jit(solution)/shard_map/all_to_all | solution.py:11
  135.0 347.6 %all-reduce.2.cloned.1.call-start = ((), (), s32[]{:S(2)}) async-start(), calls=%async_computation.2 | async-start | bytes 131072 | tf_op jit(solution)/shard_map/psum | solution.py:49
  135.0 9.8 %collective-permute-start.3 = (bf16[16,64,128]{2,1,0:T(8,128)(2,1)S(1)}, bf16[16,64,128]{2,1,0:T(8,128)(2,1)S(1)}, u32[]{:S(2)}, u32[]{:S(2)}) collective-permute-start(bf16[16,64,128]{2,1,0:T(8,128)(2,1)S(1)} %get-tuple-element.8), channel_id=1, source_target_pairs={{16,0},{32,16},{48,32},{64,48},{80,64},{96,80},{112,96},{128,112},... | collective-permute-start | bytes 786440 | tf_op jit(solution)/shard_map/ppermute | solution.py:19
  138.8 6.8 %collective-permute-start.2 = (bf16[16,64,128]{2,1,0:T(8,128)(2,1)S(1)}, bf16[16,64,128]{2,1,0:T(8,128)(2,1)S(1)}, u32[]{:S(2)}, u32[]{:S(2)}) collective-permute-start(bf16[16,64,128]{2,1,0:T(8,128)(2,1)S(1)} %get-tuple-element.8), channel_id=1, source_target_pairs={{0,16},{16,32},{32,48},{48,64},{64,80},{80,96},{96,112},{112,128},... | collective-permute-start | bytes 786440 | tf_op jit(solution)/shard_map/ppermute | solution.py:18
Sparse Core Ops, SparseCore 0:
  242.4 240.0 all-reduce.1
